TPU v7x, 256 devices: a whole 4x4x8 slice. The times are simulated.
256 devices in a mesh: ctx: 32 (over z, y_hi, core), head: 8 (over x, y_lo).
Axes of the slice: x: 4, y: 4 (y_hi: 2, y_lo: 2; y = y_hi * 2 + y_lo), z: 8, core: 2. Of those that a mesh axis runs over, the one named last changes fastest.
Arguments:
- queries: bfloat16 [20480, 2048], P('ctx', 'head'), may hold values from -8 to 8
- keys: bfloat16 [20480, 2048], P('ctx', 'head'), may hold values from -6 to 6
- values: bfloat16 [20480, 2048], P('ctx', 'head'), may hold values from -6 to 6
- key_weight: bfloat16 [16, 16, 128], P('head'), may hold values from -1.5 to 1.5
- value_weight: bfloat16 [16, 16, 128], P('head'), may hold values from -1.5 to 1.5
Outputs:
- attended: bfloat16 [20480, 2048], P(('ctx', 'head'))
All inputs are finite; a program needn't handle non-finite values.
Results may differ from a plain program's by a relative error of at most 0.0061.
Values may be sent and summed in bfloat16 or wider, within the bound.
No kernel may reach another device: no remote copies, remote signals or barrier semaphores. Data moves between devices by JAX's collectives and lax.ppermute only.
A program may use at most 64 MiB of HBM per device.

v0:
```python
import functools
import math

import jax
import jax.numpy as jnp
from jax import lax
from jax.experimental import pallas as pl
from jax.experimental.pallas import tpu as pltpu
from jax.sharding import PartitionSpec as P


vmem_spec = pl.BlockSpec(memory_space=pltpu.VMEM)


def z_perm(size, target):
    return [(i, target(i // 4) % (size // 4) * 4 + i % 4) for i in range(size)]


def bit_perm(size, bit):
    return [(i, i ^ (1 << bit)) for i in range(size)]


def prepare_kernel(keys, values, key_weight, value_weight, lead, key_tail, low_values, high_values, *scratch):
    weights, sems = scratch[:2], scratch[2]
    cut, half = keys.shape[0] - key_tail.shape[0], low_values.shape[0]
    copies = [
        pltpu.make_async_copy(source, target, sems.at[index])
        for index, (source, target) in enumerate(
            (
                (key_weight, weights[0]),
                (value_weight, weights[1]),
                (keys.at[:cut], lead.at[:cut]),
                (keys.at[cut:], key_tail),
                (values.at[:half], low_values),
                (values.at[half:], high_values),
            )
        )
    ]
    for copy in copies:
        copy.start()
    for copy in copies:
        copy.wait()
    row = cut
    for weight, blocks in zip(weights, ((lead.at[:cut], key_tail), (low_values, high_values))):
        head_count, group, width = weight.shape
        for block in blocks:
            groups = block.shape[0] // group
            for head in range(head_count):
                lanes = slice(head * width, (head + 1) * width)
                grouped = block[:, lanes].astype(jnp.float32).reshape(groups, group, width)
                summed = jnp.sum(grouped * weight[head].astype(jnp.float32)[None], axis=1)
                lead[row : row + groups, lanes] = summed.astype(lead.dtype)
            row += groups


def prepare(keys, values, key_weight, value_weight, cut, half):
    rows, channels = keys.shape
    groups = rows // key_weight.shape[1]
    shapes = [(cut + 2 * groups, channels), (rows - cut, channels), (half, channels), (rows - half, channels)]
    return pl.pallas_call(
        prepare_kernel,
        name="prepare",
        out_shape=[jax.ShapeDtypeStruct(shape, keys.dtype) for shape in shapes],
        in_specs=[pl.BlockSpec(memory_space=pltpu.HBM)] * 4,
        out_specs=[vmem_spec] * 4,
        scratch_shapes=[
            pltpu.VMEM(key_weight.shape, key_weight.dtype),
            pltpu.VMEM(value_weight.shape, value_weight.dtype),
            pltpu.SemaphoreType.DMA((6,)),
        ],
        compiler_params=pltpu.CompilerParams(vmem_limit_bytes=16 << 20),
        cost_estimate=pl.CostEstimate(flops=4 * rows * channels, bytes_accessed=4 * rows * channels, transcendentals=0),
    )(keys, values, key_weight, value_weight)


def attend_kernel(layout, first, last, width, *refs):
    queries, rest = refs[0], list(refs[1:])
    sets = []
    for count in layout:
        if isinstance(count, int):
            sets.append(([r.at[0] for r in rest[:count]], [r.at[1] for r in rest[:count]]))
            rest = rest[count:]
        else:
            keys_in, values_in = count
            taken = [r.at[:n] for r, n in zip(rest, keys_in + values_in)]
            sets.append((taken[: len(keys_in)], taken[len(keys_in) :]))
            rest = rest[len(taken) :]
    if not first:
        top_in, total_in, sum_in, rest = *rest[:3], rest[3:]
    heads = queries.shape[1] // width
    factor = math.log2(math.e) / math.sqrt(width)
    for head in range(heads):
        lanes = slice(head * width, (head + 1) * width)
        join = lambda blocks: jnp.concatenate([b[:, lanes] for b in blocks], 0) if len(blocks) > 1 else blocks[0][:, lanes]
        query = queries[:, lanes]
        scores = [
            lax.dot_general(query, join(k), (((1,), (1,)), ((), ())), preferred_element_type=jnp.float32)
            for k, _ in sets
        ]
        top = functools.reduce(jnp.maximum, [jnp.max(s, axis=1, keepdims=True) for s in scores])
        if not first:
            top_before = top_in[:, lanes][:, :1]
            top = jnp.maximum(top, top_before)
        weights = [jnp.exp2((s - top) * factor) for s in scores]
        total = sum(jnp.sum(w, axis=1, keepdims=True) for w in weights)
        summed = sum(
            jnp.dot(w.astype(jnp.bfloat16), join(v), preferred_element_type=jnp.float32)
            for w, (_, v) in zip(weights, sets)
        )
        if not first:
            decay = jnp.exp2((top_before - top) * factor)
            total = total + decay * total_in[:, lanes][:, :1]
            summed = summed + decay * sum_in[:, lanes]
        if last:
            rest[0][:, lanes] = (summed * (1.0 / total)).astype(jnp.bfloat16)
        else:
            rest[0][:, lanes] = jnp.broadcast_to(top, summed.shape)
            rest[1][:, lanes] = jnp.broadcast_to(total, summed.shape)
            rest[2][:, lanes] = summed


def attend(carried, queries, sets, width, last=False):
    rows, channels = queries.shape
    layout, operands, key_count = [], [queries], 0
    for entry in sets:
        if isinstance(entry, tuple):
            layout.append(tuple([n for _, n in blocks] for blocks in entry))
            operands += [x for blocks in entry for x, _ in blocks]
            key_count += sum(layout[-1][0])
        else:
            layout.append(len(entry))
            operands += entry
            key_count += sum(k.shape[1] for k in entry)
    operands += carried or ()
    if last:
        out_shape = jax.ShapeDtypeStruct((rows, channels), jnp.bfloat16)
        out_specs = vmem_spec
    else:
        out_shape = [jax.ShapeDtypeStruct((rows, channels), jnp.float32)] * 3
        out_specs = [vmem_spec] * 3
    return pl.pallas_call(
        functools.partial(attend_kernel, layout, carried is None, last, width),
        name="attend",
        out_shape=out_shape,
        in_specs=[vmem_spec] * len(operands),
        out_specs=out_specs,
        compiler_params=pltpu.CompilerParams(vmem_limit_bytes=24 << 20),
        cost_estimate=pl.CostEstimate(
            flops=8 * rows * key_count * channels,
            bytes_accessed=4 * key_count * channels + 4 * rows * channels,
            transcendentals=rows * key_count * channels // width,
        ),
    )(*operands)


def move(rows, pairs):
    return lax.ppermute(rows, "ctx", pairs)


def body(queries, keys, values, key_weight, value_weight):
    width = key_weight.shape[2]
    size = lax.axis_size("ctx")
    block, channels = keys.shape
    cut, half, groups = key_cut, value_cut, block // key_weight.shape[1]
    core, y_side, z_one, z_two = (bit_perm(size, bit) for bit in range(4))
    z_side = z_perm(size, lambda z: z + 2 if z & 2 else z - 2)
    z_odd = z_perm(size, lambda z: z + 1 if z & 1 else z - 1)

    lead, key_tail, low_values, high_values = prepare(keys, values, key_weight, value_weight, cut, half)
    own_rows = lead[cut:]
    two = [move(lead, z_two), move(low_values, z_two), move(key_tail, z_two), move(high_values, z_two)]
    four = [move(jnp.concatenate([two[0], own_rows], 0), z_side)]
    four += [move(two[i], z_side) for i in range(1, 4)]
    one = move(keys, z_one), move(values, z_one)
    twin = move(keys, core), move(values, core)
    side = move(keys, y_side), move(values, y_side)

    stacked = [x.reshape(2, groups, channels) for x in (own_rows, two[0][cut:], four[0][cut : cut + 2 * groups], four[0][cut + 2 * groups :])]
    even = jnp.concatenate(stacked, 1)
    odd = move(even, z_odd)
    even_side, odd_side = move(even, y_side), move(odd, y_side)
    comp_even = [even, even_side, move(even, core), move(even_side, core)]
    comp_odd = [odd, odd_side, move(odd, core), move(odd_side, core)]

    whole = lambda *blocks: [(x, block) for x in blocks]
    parts = lambda c: ([(c[0], cut), (c[2], block - cut)], [(c[1], half), (c[3], block - half)])
    stages = {
        "own": [parts((lead, low_values, key_tail, high_values)), (whole(twin[0]), whole(twin[1]))],
        "side": [(whole(side[0]), whole(side[1]))],
        "even": [comp_even],
        "odd": [comp_odd, parts(two)],
        "one": [(whole(one[0]), whole(one[1]))],
        "rest": [parts(four)],
    }
    carried = None
    for name, sets in stages.items():
        carried = attend(carried, queries, sets, width, last=name == "rest")
    return lax.all_to_all(carried, "head", split_axis=0, concat_axis=1, tiled=True)


key_cut = 128
value_cut = 384


def solution(mesh):
    in_specs = (
        P("ctx", "head"),
        P("ctx", "head"),
        P("ctx", "head"),
        P("head", None, None),
        P("head", None, None),
    )
    out_specs = P(("ctx", "head"), None)

    return jax.shard_map(body, mesh=mesh, in_specs=in_specs, out_specs=out_specs, check_vma=False)
```

profile of v0, /device:TPU:16, one launch (start us, length us, event | category | flops | bytes accessed | tf_op | source)
XLA Modules:
  0.0 116.8 jit_solution(5871826209943091695)
XLA Ops:
  0.0 0.0 copy-start.1
  0.0 0.7 copy-done.1
  0.7 0.0 copy-start.2
  0.7 0.7 copy-done.2
  1.4 1.5 %prepare.1 = (bf16[208,256]{1,0:T(8,128)(2,1)S(1)}, bf16[512,256]{1,0:T(8,128)(2,1)S(1)}, bf16[384,256]{1,0:T(8,128)(2,1)S(1)}, bf16[256,256]{1,0:T(8,128)(2,1)S(1)}) custom-call(bf16[640,256]{1,0:T(8,128)(2,1)} %keys.1, bf16[640,256]{1,0:T(8,128)(2,1)} %values.1, bf16[2,16,128]{2,1,0:T(8,128)(2,1)S(1)} %copy-done.1, bf16[2,16,128]{2,1,0:T(8,128)(2,1)S(1)} %copy-done.2), custom_call_target="tpu_custom_call" | custom-call | flops 655360 | bytes 655360 | tf_op jit(solution)/shard_map/prepare/pallas_call | solution.py:60
  2.9 3.4 %collective-permute-start = (bf16[208,256]{1,0:T(8,128)(2,1)S(1)}, bf16[208,256]{1,0:T(8,128)(2,1)S(1)}, u32[]{:S(2)}, u32[]{:S(2)}) collective-permute-start(bf16[208,256]{1,0:T(8,128)(2,1)S(1)} %get-tuple-element.24.refs_1_), channel_id=1, source_target_pairs={{0,64},{8,72},{16,80},{24,88},{32,96},{40,104},{48,112},{56,120},{... | collective-permute-start | bytes 319496 | tf_op jit(solution)/shard_map/ppermute | solution.py:157
  6.2 5.2 %collective-permute-done.refs_5_ = bf16[208,256]{1,0:T(8,128)(2,1)S(1)} collective-permute-done((bf16[208,256]{1,0:T(8,128)(2,1)S(1)}, bf16[208,256]{1,0:T(8,128)(2,1)S(1)}, u32[]{:S(2)}, u32[]{:S(2)}) %collective-permute-start) | collective-permute-done | bytes 106528 | tf_op jit(solution)/shard_map/ppermute | solution.py:157
  11.5 0.0 copy-start
  11.5 3.8 %collective-permute-start.1 = (bf16[288,256]{1,0:T(8,128)(2,1)S(1)}, bf16[288,256]{1,0:T(8,128)(2,1)S(1)}, u32[]{:S(2)}, u32[]{:S(2)}) collective-permute-start(bf16[288,256]{1,0:T(8,128)(2,1)S(1)} %pad_maximum_fusion.1), channel_id=1, source_target_pairs={{0,192},{8,200},{16,208},{24,216},{32,224},{40,232},{48,240},{56,2... | collective-permute-start | bytes 442376 | tf_op jit(solution)/shard_map/ppermute | solution.py:157
  15.3 0.0 collective-permute-start.19
  15.3 0.5 collective-permute-start.20
  15.9 3.4 %collective-permute-start.2 = (bf16[512,256]{1,0:T(8,128)(2,1)S(1)}, bf16[512,256]{1,0:T(8,128)(2,1)S(1)}, u32[]{:S(2)}, u32[]{:S(2)}) collective-permute-start(bf16[512,256]{1,0:T(8,128)(2,1)S(1)} %get-tuple-element.25.refs_2_), channel_id=1, source_target_pairs={{0,64},{8,72},{16,80},{24,88},{32,96},{40,104},{48,112},{56,120},{... | collective-permute-start | bytes 786440 | tf_op jit(solution)/shard_map/ppermute | solution.py:157
  19.2 0.0 collective-permute-start.4
  19.3 0.7 collective-permute-done.1.refs_1_
  19.9 5.6 %collective-permute-start.6 = (bf16[256,256]{1,0:T(8,128)(2,1)S(1)}, bf16[256,256]{1,0:T(8,128)(2,1)S(1)}, u32[]{:S(2)}, u32[]{:S(2)}) collective-permute-start(bf16[256,256]{1,0:T(8,128)(2,1)S(1)} %get-tuple-element.27.refs_4_), channel_id=1, source_target_pairs={{0,64},{8,72},{16,80},{24,88},{32,96},{40,104},{48,112},{56,120},{... | collective-permute-start | bytes 393224 | tf_op jit(solution)/shard_map/ppermute | solution.py:157
  25.6 19.9 %collective-permute-done.6.refs_8_ = bf16[256,256]{1,0:T(8,128)(2,1)S(1)} collective-permute-done((bf16[256,256]{1,0:T(8,128)(2,1)S(1)}, bf16[256,256]{1,0:T(8,128)(2,1)S(1)}, u32[]{:S(2)}, u32[]{:S(2)}) %collective-permute-start.6) | collective-permute-done | bytes 131104 | tf_op jit(solution)/shard_map/ppermute | solution.py:157
  45.4 0.3 collective-permute-start.17
  45.8 0.0 collective-permute-done.4.refs_7_
  45.8 3.2 %collective-permute-start.18 = (bf16[640,256]{1,0:T(8,128)(2,1)}, bf16[640,256]{1,0:T(8,128)(2,1)S(1)}, u32[]{:S(2)}, u32[]{:S(2)}) collective-permute-start(bf16[640,256]{1,0:T(8,128)(2,1)} %values.1), channel_id=1, source_target_pairs={{0,16},{8,24},{16,0},{24,8},{32,48},{40,56},{48,32},{56,40},{64,80... | collective-permute-start | bytes 983048 | tf_op jit(solution)/shard_map/ppermute | solution.py:157
  49.0 0.0 collective-permute-done.2.refs_6_
  49.0 0.9 collective-permute-start.10
  49.9 0.0 collective-permute-done.19.refs_5_
  49.9 0.3 collective-permute-start.14
  50.3 0.0 collective-permute-done.20.refs_6_
  50.3 0.0 collective-permute-start.15
  50.3 5.3 %collective-permute-done.10.refs_1_ = bf16[2,160,256]{2,1,0:T(8,128)(2,1)S(1)} collective-permute-done((bf16[2,160,256]{2,1,0:T(8,128)(2,1)S(1)}, bf16[2,160,256]{2,1,0:T(8,128)(2,1)S(1)}, u32[]{:S(2)}, u32[]{:S(2)}) %collective-permute-start.10) | collective-permute-done | bytes 163872 | tf_op jit(solution)/shard_map/ppermute | solution.py:157
  55.6 0.3 collective-permute-start.11
  55.9 1.8 %collective-permute-done.17.refs_1_ = bf16[640,256]{1,0:T(8,128)(2,1)S(1)} collective-permute-done((bf16[640,256]{1,0:T(8,128)(2,1)}, bf16[640,256]{1,0:T(8,128)(2,1)S(1)}, u32[]{:S(2)}, u32[]{:S(2)}) %collective-permute-start.17) | collective-permute-done | bytes 327712 | tf_op jit(solution)/shard_map/ppermute | solution.py:157
  57.7 0.0 collective-permute-start.8
  57.7 7.0 %collective-permute-done.18.refs_2_ = bf16[640,256]{1,0:T(8,128)(2,1)S(1)} collective-permute-done((bf16[640,256]{1,0:T(8,128)(2,1)}, bf16[640,256]{1,0:T(8,128)(2,1)S(1)}, u32[]{:S(2)}, u32[]{:S(2)}) %collective-permute-start.18) | collective-permute-done | bytes 327712 | tf_op jit(solution)/shard_map/ppermute | solution.py:157
  64.7 0.0 collective-permute-start.9
  64.7 3.5 %collective-permute-done.14.refs_2_ = bf16[2,160,256]{2,1,0:T(8,128)(2,1)S(1)} collective-permute-done((bf16[2,160,256]{2,1,0:T(8,128)(2,1)S(1)}, bf16[2,160,256]{2,1,0:T(8,128)(2,1)S(1)}, u32[]{:S(2)}, u32[]{:S(2)}) %collective-permute-start.14) | collective-permute-done | bytes 163872 | tf_op jit(solution)/shard_map/ppermute | solution.py:157
  68.2 0.0 collective-permute-start.12
  68.2 0.0 collective-permute-done.15.refs_3_
  68.3 0.5 collective-permute-start.16
  68.8 1.5 %collective-permute-done.11.refs_2_ = bf16[2,160,256]{2,1,0:T(8,128)(2,1)S(1)} collective-permute-done((bf16[2,160,256]{2,1,0:T(8,128)(2,1)S(1)}, bf16[2,160,256]{2,1,0:T(8,128)(2,1)S(1)}, u32[]{:S(2)}, u32[]{:S(2)}) %collective-permute-start.11) | collective-permute-done | bytes 163872 | tf_op jit(solution)/shard_map/ppermute | solution.py:157
  70.2 0.0 collective-permute-start.13
  70.2 0.0 copy-done
  70.2 2.5 %attend.6 = (f32[640,256]{1,0:T(8,128)S(1)}, f32[640,256]{1,0:T(8,128)S(1)}, f32[640,256]{1,0:T(8,128)S(1)}) custom-call(bf16[640,256]{1,0:T(8,128)(2,1)S(1)} %copy-done, bf16[208,256]{1,0:T(8,128)(2,1)S(1)} %get-tuple-element.24.refs_1_, bf16[512,256]{1,0:T(8,128)(2,1)S(1)} %get-tuple-element.25.refs_2_, bf16[384,256]{1,0:T(8,128)(2,1)S(1)} %get-tuple-element.26.refs_3_, ...), custom_call_target="tpu_custom_call" | custom-call | flops 1677721600 | bytes 1966080 | tf_op jit(solution)/shard_map/attend/pallas_call | solution.py:141
  72.7 2.1 %attend.7 = (f32[640,256]{1,0:T(8,128)S(1)}, f32[640,256]{1,0:T(8,128)S(1)}, f32[640,256]{1,0:T(8,128)S(1)}) custom-call(bf16[640,256]{1,0:T(8,128)(2,1)S(1)} %copy-done, bf16[640,256]{1,0:T(8,128)(2,1)S(1)} %collective-permute-done.17.refs_1_, bf16[640,256]{1,0:T(8,128)(2,1)S(1)} %collective-permute-done.18.refs_2_, ...), custom_call_target="tpu_custom_call" | custom-call | flops 838860800 | bytes 1310720 | tf_op jit(solution)/shard_map/attend/pallas_call | solution.py:141
  74.8 0.0 collective-permute-done.16.refs_4_
  74.8 0.1 collective-permute-start.3
  74.9 2.1 %attend.8 = (f32[640,256]{1,0:T(8,128)S(1)}, f32[640,256]{1,0:T(8,128)S(1)}, f32[640,256]{1,0:T(8,128)S(1)}) custom-call(bf16[640,256]{1,0:T(8,128)(2,1)S(1)} %copy-done, bf16[2,160,256]{2,1,0:T(8,128)(2,1)S(1)} %pad_maximum_fusion.refs_1_, bf16[2,160,256]{2,1,0:T(8,128)(2,1)S(1)} %collective-permute-done.14.refs_2_, ...), custom_call_target="tpu_custom_call" | custom-call | flops 838860800 | bytes 1310720 | tf_op jit(solution)/shard_map/attend/pallas_call | solution.py:141
  77.0 0.0 collective-permute-done.12.refs_3_
  77.0 4.2 %collective-permute-start.7 = (bf16[256,256]{1,0:T(8,128)(2,1)S(1)}, bf16[256,256]{1,0:T(8,128)(2,1)S(1)}, u32[]{:S(2)}, u32[]{:S(2)}) collective-permute-start(bf16[256,256]{1,0:T(8,128)(2,1)S(1)} %collective-permute-done.6.refs_8_), channel_id=1, source_target_pairs={{0,192},{8,200},{16,208},{24,216},{32,224},{40,232},{48,240},{56,2... | collective-permute-start | bytes 393224 | tf_op jit(solution)/shard_map/ppermute | solution.py:157
  81.2 0.0 collective-permute-done.13.refs_4_
  81.2 0.3 collective-permute-start.5
  81.5 2.8 %attend.9 = (f32[640,256]{1,0:T(8,128)S(1)}, f32[640,256]{1,0:T(8,128)S(1)}, f32[640,256]{1,0:T(8,128)S(1)}) custom-call(bf16[640,256]{1,0:T(8,128)(2,1)S(1)} %copy-done, bf16[2,160,256]{2,1,0:T(8,128)(2,1)S(1)} %collective-permute-done.10.refs_1_, bf16[2,160,256]{2,1,0:T(8,128)(2,1)S(1)} %collective-permute-done.11.refs_2_, ...), custom_call_target="tpu_custom_call" | custom-call | flops 1677721600 | bytes 1966080 | tf_op jit(solution)/shard_map/attend/pallas_call | solution.py:141
  84.3 0.0 collective-permute-done.8.refs_1_
  84.3 0.0 collective-permute-done.9.refs_2_
  84.3 2.1 %attend.10 = (f32[640,256]{1,0:T(8,128)S(1)}, f32[640,256]{1,0:T(8,128)S(1)}, f32[640,256]{1,0:T(8,128)S(1)}) custom-call(bf16[640,256]{1,0:T(8,128)(2,1)S(1)} %copy-done, bf16[640,256]{1,0:T(8,128)(2,1)S(1)} %collective-permute-done.8.refs_1_, bf16[640,256]{1,0:T(8,128)(2,1)S(1)} %collective-permute-done.9.refs_2_, ...), custom_call_target="tpu_custom_call" | custom-call | flops 838860800 | bytes 1310720 | tf_op jit(solution)/shard_map/attend/pallas_call | solution.py:141
  86.4 10.6 %collective-permute-done.7.refs_4_ = bf16[256,256]{1,0:T(8,128)(2,1)S(1)} collective-permute-done((bf16[256,256]{1,0:T(8,128)(2,1)S(1)}, bf16[256,256]{1,0:T(8,128)(2,1)S(1)}, u32[]{:S(2)}, u32[]{:S(2)}) %collective-permute-start.7) | collective-permute-done | bytes 131104 | tf_op jit(solution)/shard_map/ppermute | solution.py:157
  97.0 4.0 %collective-permute-done.5.refs_3_ = bf16[384,256]{1,0:T(8,128)(2,1)S(1)} collective-permute-done((bf16[384,256]{1,0:T(8,128)(2,1)S(1)}, bf16[384,256]{1,0:T(8,128)(2,1)S(1)}, u32[]{:S(2)}, u32[]{:S(2)}) %collective-permute-start.5) | collective-permute-done | bytes 196640 | tf_op jit(solution)/shard_map/ppermute | solution.py:157
  101.1 0.0 collective-permute-done.3.refs_2_
  101.1 2.1 %attend.11 = bf16[640,256]{1,0:T(8,128)(2,1)S(1)} custom-call(bf16[640,256]{1,0:T(8,128)(2,1)S(1)} %copy-done, bf16[288,256]{1,0:T(8,128)(2,1)S(1)} %collective-permute-done.1.refs_1_, bf16[512,256]{1,0:T(8,128)(2,1)S(1)} %collective-permute-done.3.refs_2_, bf16[384,256]{1,0:T(8,128)(2,1)S(1)} %collective-permute-done.5.refs_3_, ...), custom_call_target="tpu_custom_call" | custom-call | flops 838860800 | bytes 1310720 | tf_op jit(solution)/shard_map/attend/pallas_call | solution.py:141
  103.1 12.9 %all_to_all.19 = bf16[8,80,256]{2,1,0:T(8,128)(2,1)S(1)} all-to-all(bf16[8,80,256]{2,1,0:T(8,128)(2,1)S(1)} %bitcast.8), channel_id=1, replica_groups=mesh['ctx'=32,'head'=8] {'head'}, dimensions={0} | all-to-all | bytes 655360 | tf_op jit(solution)/shard_map/all_to_all | solution.py:198
  116.1 0.8 copy.7
  (5 shorter events, 0.0 us)
Async XLA Ops:
  0.0 0.7 copy-start.1
  0.7 0.7 copy-start.2
  2.9 8.6 %collective-permute-start = (bf16[208,256]{1,0:T(8,128)(2,1)S(1)}, bf16[208,256]{1,0:T(8,128)(2,1)S(1)}, u32[]{:S(2)}, u32[]{:S(2)}) collective-permute-start(bf16[208,256]{1,0:T(8,128)(2,1)S(1)} %get-tuple-element.24.refs_1_), channel_id=1, source_target_pairs={{0,64},{8,72},{16,80},{24,88},{32,96},{40,104},{48,112},{56,120},{... | collective-permute-start | bytes 319496 | tf_op jit(solution)/shard_map/ppermute | solution.py:157
  11.5 58.7 %copy-start = (bf16[640,256]{1,0:T(8,128)(2,1)S(1)}, bf16[640,256]{1,0:T(8,128)(2,1)}, u32[]{:S(2)}) copy-start(bf16[640,256]{1,0:T(8,128)(2,1)} %refs_0_.11) | copy-start | bytes 983044
  11.5 8.4 %collective-permute-start.1 = (bf16[288,256]{1,0:T(8,128)(2,1)S(1)}, bf16[288,256]{1,0:T(8,128)(2,1)S(1)}, u32[]{:S(2)}, u32[]{:S(2)}) collective-permute-start(bf16[288,256]{1,0:T(8,128)(2,1)S(1)} %pad_maximum_fusion.1), channel_id=1, source_target_pairs={{0,192},{8,200},{16,208},{24,216},{32,224},{40,232},{48,240},{56,2... | collective-permute-start | bytes 442376 | tf_op jit(solution)/shard_map/ppermute | solution.py:157
  15.3 34.6 %collective-permute-start.19 = (bf16[640,256]{1,0:T(8,128)(2,1)}, bf16[640,256]{1,0:T(8,128)(2,1)S(1)}, u32[]{:S(2)}, u32[]{:S(2)}) collective-permute-start(bf16[640,256]{1,0:T(8,128)(2,1)} %keys.1), channel_id=1, source_target_pairs={{0,8},{8,0},{16,24},{24,16},{32,40},{40,32},{48,56},{56,48},{64,72... | collective-permute-start | bytes 983048 | tf_op jit(solution)/shard_map/ppermute | solution.py:157
  15.3 34.9 %collective-permute-start.20 = (bf16[640,256]{1,0:T(8,128)(2,1)}, bf16[640,256]{1,0:T(8,128)(2,1)S(1)}, u32[]{:S(2)}, u32[]{:S(2)}) collective-permute-start(bf16[640,256]{1,0:T(8,128)(2,1)} %values.1), channel_id=1, source_target_pairs={{0,8},{8,0},{16,24},{24,16},{32,40},{40,32},{48,56},{56,48},{64,72... | collective-permute-start | bytes 983048 | tf_op jit(solution)/shard_map/ppermute | solution.py:157
  15.9 33.1 %collective-permute-start.2 = (bf16[512,256]{1,0:T(8,128)(2,1)S(1)}, bf16[512,256]{1,0:T(8,128)(2,1)S(1)}, u32[]{:S(2)}, u32[]{:S(2)}) collective-permute-start(bf16[512,256]{1,0:T(8,128)(2,1)S(1)} %get-tuple-element.25.refs_2_), channel_id=1, source_target_pairs={{0,64},{8,72},{16,80},{24,88},{32,96},{40,104},{48,112},{56,120},{... | collective-permute-start | bytes 786440 | tf_op jit(solution)/shard_map/ppermute | solution.py:157
  19.2 26.5 %collective-permute-start.4 = (bf16[384,256]{1,0:T(8,128)(2,1)S(1)}, bf16[384,256]{1,0:T(8,128)(2,1)S(1)}, u32[]{:S(2)}, u32[]{:S(2)}) collective-permute-start(bf16[384,256]{1,0:T(8,128)(2,1)S(1)} %get-tuple-element.26.refs_3_), channel_id=1, source_target_pairs={{0,64},{8,72},{16,80},{24,88},{32,96},{40,104},{48,112},{56,120},{... | collective-permute-start | bytes 589832 | tf_op jit(solution)/shard_map/ppermute | solution.py:157
  19.9 25.5 %collective-permute-start.6 = (bf16[256,256]{1,0:T(8,128)(2,1)S(1)}, bf16[256,256]{1,0:T(8,128)(2,1)S(1)}, u32[]{:S(2)}, u32[]{:S(2)}) collective-permute-start(bf16[256,256]{1,0:T(8,128)(2,1)S(1)} %get-tuple-element.27.refs_4_), channel_id=1, source_target_pairs={{0,64},{8,72},{16,80},{24,88},{32,96},{40,104},{48,112},{56,120},{... | collective-permute-start | bytes 393224 | tf_op jit(solution)/shard_map/ppermute | solution.py:157
  45.4 12.3 %collective-permute-start.17 = (bf16[640,256]{1,0:T(8,128)(2,1)}, bf16[640,256]{1,0:T(8,128)(2,1)S(1)}, u32[]{:S(2)}, u32[]{:S(2)}) collective-permute-start(bf16[640,256]{1,0:T(8,128)(2,1)} %keys.1), channel_id=1, source_target_pairs={{0,16},{8,24},{16,0},{24,8},{32,48},{40,56},{48,32},{56,40},{64,80... | collective-permute-start | bytes 983048 | tf_op jit(solution)/shard_map/ppermute | solution.py:157
  45.8 19.0 %collective-permute-start.18 = (bf16[640,256]{1,0:T(8,128)(2,1)}, bf16[640,256]{1,0:T(8,128)(2,1)S(1)}, u32[]{:S(2)}, u32[]{:S(2)}) collective-permute-start(bf16[640,256]{1,0:T(8,128)(2,1)} %values.1), channel_id=1, source_target_pairs={{0,16},{8,24},{16,0},{24,8},{32,48},{40,56},{48,32},{56,40},{64,80... | collective-permute-start | bytes 983048 | tf_op jit(solution)/shard_map/ppermute | solution.py:157
  49.0 6.6 %collective-permute-start.10 = (bf16[2,160,256]{2,1,0:T(8,128)(2,1)S(1)}, bf16[2,160,256]{2,1,0:T(8,128)(2,1)S(1)}, u32[]{:S(2)}, u32[]{:S(2)}) collective-permute-start(bf16[2,160,256]{2,1,0:T(8,128)(2,1)S(1)} %pad_maximum_fusion.refs_1_), channel_id=1, source_target_pairs={{0,224},{8,232},{16,240},{24,248},{32,64},{40,72},{48,80},{56,88},... | collective-permute-start | bytes 491528 | tf_op jit(solution)/shard_map/ppermute | solution.py:157
  49.9 18.3 %collective-permute-start.14 = (bf16[2,160,256]{2,1,0:T(8,128)(2,1)S(1)}, bf16[2,160,256]{2,1,0:T(8,128)(2,1)S(1)}, u32[]{:S(2)}, u32[]{:S(2)}) collective-permute-start(bf16[2,160,256]{2,1,0:T(8,128)(2,1)S(1)} %pad_maximum_fusion.refs_1_), channel_id=1, source_target_pairs={{0,16},{8,24},{16,0},{24,8},{32,48},{40,56},{48,32},{56,40},{64,80... | collective-permute-start | bytes 491528 | tf_op jit(solution)/shard_map/ppermute | solution.py:157
  50.3 18.0 %collective-permute-start.15 = (bf16[2,160,256]{2,1,0:T(8,128)(2,1)S(1)}, bf16[2,160,256]{2,1,0:T(8,128)(2,1)S(1)}, u32[]{:S(2)}, u32[]{:S(2)}) collective-permute-start(bf16[2,160,256]{2,1,0:T(8,128)(2,1)S(1)} %pad_maximum_fusion.refs_1_), channel_id=1, source_target_pairs={{0,8},{8,0},{16,24},{24,16},{32,40},{40,32},{48,56},{56,48},{64,72... | collective-permute-start | bytes 491528 | tf_op jit(solution)/shard_map/ppermute | solution.py:157
  55.6 14.6 %collective-permute-start.11 = (bf16[2,160,256]{2,1,0:T(8,128)(2,1)S(1)}, bf16[2,160,256]{2,1,0:T(8,128)(2,1)S(1)}, u32[]{:S(2)}, u32[]{:S(2)}) collective-permute-start(bf16[2,160,256]{2,1,0:T(8,128)(2,1)S(1)} %collective-permute-done.10.refs_1_), channel_id=1, source_target_pairs={{0,16},{8,24},{16,0},{24,8},{32,48},{40,56},{48,32},{56,40},{64,80... | collective-permute-start | bytes 491528 | tf_op jit(solution)/shard_map/ppermute | solution.py:157
  57.7 26.6 %collective-permute-start.8 = (bf16[640,256]{1,0:T(8,128)(2,1)}, bf16[640,256]{1,0:T(8,128)(2,1)S(1)}, u32[]{:S(2)}, u32[]{:S(2)}) collective-permute-start(bf16[640,256]{1,0:T(8,128)(2,1)} %keys.1), channel_id=1, source_target_pairs={{0,32},{8,40},{16,48},{24,56},{32,0},{40,8},{48,16},{56,24},{64,96... | collective-permute-start | bytes 983048 | tf_op jit(solution)/shard_map/ppermute | solution.py:157
  64.7 19.6 %collective-permute-start.9 = (bf16[640,256]{1,0:T(8,128)(2,1)}, bf16[640,256]{1,0:T(8,128)(2,1)S(1)}, u32[]{:S(2)}, u32[]{:S(2)}) collective-permute-start(bf16[640,256]{1,0:T(8,128)(2,1)} %values.1), channel_id=1, source_target_pairs={{0,32},{8,40},{16,48},{24,56},{32,0},{40,8},{48,16},{56,24},{64,96... | collective-permute-start | bytes 983048 | tf_op jit(solution)/shard_map/ppermute | solution.py:157
  68.2 8.7 %collective-permute-start.12 = (bf16[2,160,256]{2,1,0:T(8,128)(2,1)S(1)}, bf16[2,160,256]{2,1,0:T(8,128)(2,1)S(1)}, u32[]{:S(2)}, u32[]{:S(2)}) collective-permute-start(bf16[2,160,256]{2,1,0:T(8,128)(2,1)S(1)} %collective-permute-done.10.refs_1_), channel_id=1, source_target_pairs={{0,8},{8,0},{16,24},{24,16},{32,40},{40,32},{48,56},{56,48},{64,72... | collective-permute-start | bytes 491528 | tf_op jit(solution)/shard_map/ppermute | solution.py:157
  68.3 6.5 %collective-permute-start.16 = (bf16[2,160,256]{2,1,0:T(8,128)(2,1)S(1)}, bf16[2,160,256]{2,1,0:T(8,128)(2,1)S(1)}, u32[]{:S(2)}, u32[]{:S(2)}) collective-permute-start(bf16[2,160,256]{2,1,0:T(8,128)(2,1)S(1)} %collective-permute-done.14.refs_2_), channel_id=1, source_target_pairs={{0,8},{8,0},{16,24},{24,16},{32,40},{40,32},{48,56},{56,48},{64,72... | collective-permute-start | bytes 491528 | tf_op jit(solution)/shard_map/ppermute | solution.py:157
  70.2 11.0 %collective-permute-start.13 = (bf16[2,160,256]{2,1,0:T(8,128)(2,1)S(1)}, bf16[2,160,256]{2,1,0:T(8,128)(2,1)S(1)}, u32[]{:S(2)}, u32[]{:S(2)}) collective-permute-start(bf16[2,160,256]{2,1,0:T(8,128)(2,1)S(1)} %collective-permute-done.11.refs_2_), channel_id=1, source_target_pairs={{0,8},{8,0},{16,24},{24,16},{32,40},{40,32},{48,56},{56,48},{64,72... | collective-permute-start | bytes 491528 | tf_op jit(solution)/shard_map/ppermute | solution.py:157
  74.8 26.3 %collective-permute-start.3 = (bf16[512,256]{1,0:T(8,128)(2,1)S(1)}, bf16[512,256]{1,0:T(8,128)(2,1)S(1)}, u32[]{:S(2)}, u32[]{:S(2)}) collective-permute-start(bf16[512,256]{1,0:T(8,128)(2,1)S(1)} %collective-permute-done.2.refs_6_), channel_id=1, source_target_pairs={{0,192},{8,200},{16,208},{24,216},{32,224},{40,232},{48,240},{56,2... | collective-permute-start | bytes 786440 | tf_op jit(solution)/shard_map/ppermute | solution.py:157
  77.0 20.1 %collective-permute-start.7 = (bf16[256,256]{1,0:T(8,128)(2,1)S(1)}, bf16[256,256]{1,0:T(8,128)(2,1)S(1)}, u32[]{:S(2)}, u32[]{:S(2)}) collective-permute-start(bf16[256,256]{1,0:T(8,128)(2,1)S(1)} %collective-permute-done.6.refs_8_), channel_id=1, source_target_pairs={{0,192},{8,200},{16,208},{24,216},{32,224},{40,232},{48,240},{56,2... | collective-permute-start | bytes 393224 | tf_op jit(solution)/shard_map/ppermute | solution.py:157
  81.2 19.9 %collective-permute-start.5 = (bf16[384,256]{1,0:T(8,128)(2,1)S(1)}, bf16[384,256]{1,0:T(8,128)(2,1)S(1)}, u32[]{:S(2)}, u32[]{:S(2)}) collective-permute-start(bf16[384,256]{1,0:T(8,128)(2,1)S(1)} %collective-permute-done.4.refs_7_), channel_id=1, source_target_pairs={{0,192},{8,200},{16,208},{24,216},{32,224},{40,232},{48,240},{56,2... | collective-permute-start | bytes 589832 | tf_op jit(solution)/shard_map/ppermute | solution.py:157
where the time goes:
time: 119 us; the launch traced here: 117 us
  waiting for transfers between devices  59.5 us (50%)
  starting transfers between devices  27 us (23%)
  Pallas kernels  15 us (13%)
  blocking collectives  12.9 us (11%)
  local copies, waits for them, and re-layouts  2.16 us (2%)
    ppermute x21, waiting for transfers between devices, move(): return lax.ppermute(rows, 'ctx', pairs)  59.5 us
    ppermute x21, starting transfers between devices, move(): return lax.ppermute(rows, 'ctx', pairs)  27 us
    pallas_call x6, Pallas kernels, attend(): pl.pallas_call(functools.partial(attend_kernel, layout, carried is None,...  13.5 us
    all_to_all x1, blocking collectives, body(): lax.all_to_all(carried, 'head', split_axis=0, concat_axis=1, tiled=True)  12.9 us
  transfers between devices with their start and end apart: 21, of which 10 were waited for; matrix products, arithmetic and copies ran while one was open for 0% of the time, Pallas kernels for 10%

commit v1 on v0

--- a/solution.py
+++ b/solution.py
@@ -28,9 +28,9 @@
         for index, (source, target) in enumerate(
             (
                 (key_weight, weights[0]),
-                (value_weight, weights[1]),
                 (keys.at[:cut], lead.at[:cut]),
                 (keys.at[cut:], key_tail),
+                (value_weight, weights[1]),
                 (values.at[:half], low_values),
                 (values.at[half:], high_values),
             )
@@ -38,10 +38,11 @@
     ]
     for copy in copies:
         copy.start()
-    for copy in copies:
-        copy.wait()
     row = cut
-    for weight, blocks in zip(weights, ((lead.at[:cut], key_tail), (low_values, high_values))):
+    for side, blocks in enumerate(((lead.at[:cut], key_tail), (low_values, high_values))):
+        for copy in copies[3 * side : 3 * side + 3]:
+            copy.wait()
+        weight = weights[side]
         head_count, group, width = weight.shape
         for block in blocks:
             groups = block.shape[0] // group
@@ -70,7 +71,7 @@
         ],
         compiler_params=pltpu.CompilerParams(vmem_limit_bytes=16 << 20),
         cost_estimate=pl.CostEstimate(flops=4 * rows * channels, bytes_accessed=4 * rows * channels, transcendentals=0),
-    )(keys, values, key_weight, value_weight)
+    )(keys, values, *(pltpu.with_memory_space_constraint(w, pltpu.HBM) for w in (key_weight, value_weight)))
 
 
 def attend_kernel(layout, first, last, width, *refs):

time: 119 us -> 117 us (0.983)
  local copies, waits for them, and re-layouts: 2.16 us -> 0.77 us
    unnamed x6 -> x2, local copies, waits for them, and re-layouts: 1.4 us -> 0.01 us
where the time goes in v1:
time: 117 us; the launch traced here: 115 us
  waiting for transfers between devices  59.6 us (51%)
  starting transfers between devices  27 us (23%)
  Pallas kernels  14.9 us (13%)
  blocking collectives  12.9 us (11%)
    ppermute x21, waiting for transfers between devices, move(): return lax.ppermute(rows, 'ctx', pairs)  59.6 us
    ppermute x21, starting transfers between devices, move(): return lax.ppermute(rows, 'ctx', pairs)  27 us
    pallas_call x6, Pallas kernels, attend(): pl.pallas_call(functools.partial(attend_kernel, layout, carried is None,...  13.5 us
    all_to_all x1, blocking collectives, body(): lax.all_to_all(carried, 'head', split_axis=0, concat_axis=1, tiled=True)  12.9 us
  transfers between devices with their start and end apart: 21, of which 10 were waited for; matrix products, arithmetic and copies ran while one was open for 0% of the time, Pallas kernels for 10%

profile of v1, /device:TPU:16, one launch (start us, length us, event | category | flops | bytes accessed | tf_op | source)
XLA Modules:
  0.0 115.3 jit_solution(15774515953958724418)
XLA Ops:
  0.0 1.4 %prepare.1 = (bf16[208,256]{1,0:T(8,128)(2,1)S(1)}, bf16[512,256]{1,0:T(8,128)(2,1)S(1)}, bf16[384,256]{1,0:T(8,128)(2,1)S(1)}, bf16[256,256]{1,0:T(8,128)(2,1)S(1)}) custom-call(bf16[640,256]{1,0:T(8,128)(2,1)} %keys.1, bf16[640,256]{1,0:T(8,128)(2,1)} %values.1, bf16[2,16,128]{2,1,0:T(8,128)(2,1)} %key_weight.1, bf16[2,16,128]{2,1,0:T(8,128)(2,1)} %value_weight.1), custom_call_target="tpu_custom_call" | custom-call | flops 655360 | bytes 655360 | tf_op jit(solution)/shard_map/prepare/pallas_call | solution.py:61
  1.4 3.4 %collective-permute-start = (bf16[208,256]{1,0:T(8,128)(2,1)S(1)}, bf16[208,256]{1,0:T(8,128)(2,1)S(1)}, u32[]{:S(2)}, u32[]{:S(2)}) collective-permute-start(bf16[208,256]{1,0:T(8,128)(2,1)S(1)} %get-tuple-element.24.refs_1_), channel_id=1, source_target_pairs={{0,64},{8,72},{16,80},{24,88},{32,96},{40,104},{48,112},{56,120},{... | collective-permute-start | bytes 319496 | tf_op jit(solution)/shard_map/ppermute | solution.py:158
  4.7 5.2 %collective-permute-done.refs_5_ = bf16[208,256]{1,0:T(8,128)(2,1)S(1)} collective-permute-done((bf16[208,256]{1,0:T(8,128)(2,1)S(1)}, bf16[208,256]{1,0:T(8,128)(2,1)S(1)}, u32[]{:S(2)}, u32[]{:S(2)}) %collective-permute-start) | collective-permute-done | bytes 106528 | tf_op jit(solution)/shard_map/ppermute | solution.py:158
  10.0 0.0 copy-start
  10.0 3.8 %collective-permute-start.1 = (bf16[288,256]{1,0:T(8,128)(2,1)S(1)}, bf16[288,256]{1,0:T(8,128)(2,1)S(1)}, u32[]{:S(2)}, u32[]{:S(2)}) collective-permute-start(bf16[288,256]{1,0:T(8,128)(2,1)S(1)} %pad_maximum_fusion.1), channel_id=1, source_target_pairs={{0,192},{8,200},{16,208},{24,216},{32,224},{40,232},{48,240},{56,2... | collective-permute-start | bytes 442376 | tf_op jit(solution)/shard_map/ppermute | solution.py:158
  13.8 0.0 collective-permute-start.19
  13.8 0.5 collective-permute-start.20
  14.4 3.4 %collective-permute-start.2 = (bf16[512,256]{1,0:T(8,128)(2,1)S(1)}, bf16[512,256]{1,0:T(8,128)(2,1)S(1)}, u32[]{:S(2)}, u32[]{:S(2)}) collective-permute-start(bf16[512,256]{1,0:T(8,128)(2,1)S(1)} %get-tuple-element.25.refs_2_), channel_id=1, source_target_pairs={{0,64},{8,72},{16,80},{24,88},{32,96},{40,104},{48,112},{56,120},{... | collective-permute-start | bytes 786440 | tf_op jit(solution)/shard_map/ppermute | solution.py:158
  17.7 0.0 collective-permute-start.4
  17.8 0.7 collective-permute-done.1.refs_1_
  18.4 5.6 %collective-permute-start.6 = (bf16[256,256]{1,0:T(8,128)(2,1)S(1)}, bf16[256,256]{1,0:T(8,128)(2,1)S(1)}, u32[]{:S(2)}, u32[]{:S(2)}) collective-permute-start(bf16[256,256]{1,0:T(8,128)(2,1)S(1)} %get-tuple-element.27.refs_4_), channel_id=1, source_target_pairs={{0,64},{8,72},{16,80},{24,88},{32,96},{40,104},{48,112},{56,120},{... | collective-permute-start | bytes 393224 | tf_op jit(solution)/shard_map/ppermute | solution.py:158
  24.1 19.9 %collective-permute-done.6.refs_8_ = bf16[256,256]{1,0:T(8,128)(2,1)S(1)} collective-permute-done((bf16[256,256]{1,0:T(8,128)(2,1)S(1)}, bf16[256,256]{1,0:T(8,128)(2,1)S(1)}, u32[]{:S(2)}, u32[]{:S(2)}) %collective-permute-start.6) | collective-permute-done | bytes 131104 | tf_op jit(solution)/shard_map/ppermute | solution.py:158
  43.9 0.3 collective-permute-start.17
  44.3 0.0 collective-permute-done.4.refs_7_
  44.3 3.2 %collective-permute-start.18 = (bf16[640,256]{1,0:T(8,128)(2,1)}, bf16[640,256]{1,0:T(8,128)(2,1)S(1)}, u32[]{:S(2)}, u32[]{:S(2)}) collective-permute-start(bf16[640,256]{1,0:T(8,128)(2,1)} %values.1), channel_id=1, source_target_pairs={{0,16},{8,24},{16,0},{24,8},{32,48},{40,56},{48,32},{56,40},{64,80... | collective-permute-start | bytes 983048 | tf_op jit(solution)/shard_map/ppermute | solution.py:158
  47.5 0.0 collective-permute-done.2.refs_6_
  47.5 0.9 collective-permute-start.10
  48.4 0.0 collective-permute-done.19.refs_5_
  48.4 0.3 collective-permute-start.14
  48.8 0.0 collective-permute-done.20.refs_6_
  48.8 0.0 collective-permute-start.15
  48.8 5.3 %collective-permute-done.10.refs_1_ = bf16[2,160,256]{2,1,0:T(8,128)(2,1)S(1)} collective-permute-done((bf16[2,160,256]{2,1,0:T(8,128)(2,1)S(1)}, bf16[2,160,256]{2,1,0:T(8,128)(2,1)S(1)}, u32[]{:S(2)}, u32[]{:S(2)}) %collective-permute-start.10) | collective-permute-done | bytes 163872 | tf_op jit(solution)/shard_map/ppermute | solution.py:158
  54.1 0.3 collective-permute-start.11
  54.4 1.8 %collective-permute-done.17.refs_1_ = bf16[640,256]{1,0:T(8,128)(2,1)S(1)} collective-permute-done((bf16[640,256]{1,0:T(8,128)(2,1)}, bf16[640,256]{1,0:T(8,128)(2,1)S(1)}, u32[]{:S(2)}, u32[]{:S(2)}) %collective-permute-start.17) | collective-permute-done | bytes 327712 | tf_op jit(solution)/shard_map/ppermute | solution.py:158
  56.2 0.0 collective-permute-start.8
  56.2 7.0 %collective-permute-done.18.refs_2_ = bf16[640,256]{1,0:T(8,128)(2,1)S(1)} collective-permute-done((bf16[640,256]{1,0:T(8,128)(2,1)}, bf16[640,256]{1,0:T(8,128)(2,1)S(1)}, u32[]{:S(2)}, u32[]{:S(2)}) %collective-permute-start.18) | collective-permute-done | bytes 327712 | tf_op jit(solution)/shard_map/ppermute | solution.py:158
  63.2 0.0 collective-permute-start.9
  63.2 3.5 %collective-permute-done.14.refs_2_ = bf16[2,160,256]{2,1,0:T(8,128)(2,1)S(1)} collective-permute-done((bf16[2,160,256]{2,1,0:T(8,128)(2,1)S(1)}, bf16[2,160,256]{2,1,0:T(8,128)(2,1)S(1)}, u32[]{:S(2)}, u32[]{:S(2)}) %collective-permute-start.14) | collective-permute-done | bytes 163872 | tf_op jit(solution)/shard_map/ppermute | solution.py:158
  66.7 0.0 collective-permute-start.12
  66.7 0.0 collective-permute-done.15.refs_3_
  66.8 0.5 collective-permute-start.16
  67.3 1.5 %collective-permute-done.11.refs_2_ = bf16[2,160,256]{2,1,0:T(8,128)(2,1)S(1)} collective-permute-done((bf16[2,160,256]{2,1,0:T(8,128)(2,1)S(1)}, bf16[2,160,256]{2,1,0:T(8,128)(2,1)S(1)}, u32[]{:S(2)}, u32[]{:S(2)}) %collective-permute-start.11) | collective-permute-done | bytes 163872 | tf_op jit(solution)/shard_map/ppermute | solution.py:158
  68.7 0.0 collective-permute-start.13
  68.7 0.0 copy-done
  68.7 2.5 %attend.6 = (f32[640,256]{1,0:T(8,128)S(1)}, f32[640,256]{1,0:T(8,128)S(1)}, f32[640,256]{1,0:T(8,128)S(1)}) custom-call(bf16[640,256]{1,0:T(8,128)(2,1)S(1)} %copy-done, bf16[208,256]{1,0:T(8,128)(2,1)S(1)} %get-tuple-element.24.refs_1_, bf16[512,256]{1,0:T(8,128)(2,1)S(1)} %get-tuple-element.25.refs_2_, bf16[384,256]{1,0:T(8,128)(2,1)S(1)} %get-tuple-element.26.refs_3_, ...), custom_call_target="tpu_custom_call" | custom-call | flops 1677721600 | bytes 1966080 | tf_op jit(solution)/shard_map/attend/pallas_call | solution.py:142
  71.2 2.1 %attend.7 = (f32[640,256]{1,0:T(8,128)S(1)}, f32[640,256]{1,0:T(8,128)S(1)}, f32[640,256]{1,0:T(8,128)S(1)}) custom-call(bf16[640,256]{1,0:T(8,128)(2,1)S(1)} %copy-done, bf16[640,256]{1,0:T(8,128)(2,1)S(1)} %collective-permute-done.17.refs_1_, bf16[640,256]{1,0:T(8,128)(2,1)S(1)} %collective-permute-done.18.refs_2_, ...), custom_call_target="tpu_custom_call" | custom-call | flops 838860800 | bytes 1310720 | tf_op jit(solution)/shard_map/attend/pallas_call | solution.py:142
  73.3 0.0 collective-permute-done.16.refs_4_
  73.3 0.1 collective-permute-start.3
  73.4 2.1 %attend.8 = (f32[640,256]{1,0:T(8,128)S(1)}, f32[640,256]{1,0:T(8,128)S(1)}, f32[640,256]{1,0:T(8,128)S(1)}) custom-call(bf16[640,256]{1,0:T(8,128)(2,1)S(1)} %copy-done, bf16[2,160,256]{2,1,0:T(8,128)(2,1)S(1)} %pad_maximum_fusion.refs_1_, bf16[2,160,256]{2,1,0:T(8,128)(2,1)S(1)} %collective-permute-done.14.refs_2_, ...), custom_call_target="tpu_custom_call" | custom-call | flops 838860800 | bytes 1310720 | tf_op jit(solution)/shard_map/attend/pallas_call | solution.py:142
  75.5 0.0 collective-permute-done.12.refs_3_
  75.5 4.2 %collective-permute-start.7 = (bf16[256,256]{1,0:T(8,128)(2,1)S(1)}, bf16[256,256]{1,0:T(8,128)(2,1)S(1)}, u32[]{:S(2)}, u32[]{:S(2)}) collective-permute-start(bf16[256,256]{1,0:T(8,128)(2,1)S(1)} %collective-permute-done.6.refs_8_), channel_id=1, source_target_pairs={{0,192},{8,200},{16,208},{24,216},{32,224},{40,232},{48,240},{56,2... | collective-permute-start | bytes 393224 | tf_op jit(solution)/shard_map/ppermute | solution.py:158
  79.7 0.0 collective-permute-done.13.refs_4_
  79.7 0.3 collective-permute-start.5
  80.0 2.8 %attend.9 = (f32[640,256]{1,0:T(8,128)S(1)}, f32[640,256]{1,0:T(8,128)S(1)}, f32[640,256]{1,0:T(8,128)S(1)}) custom-call(bf16[640,256]{1,0:T(8,128)(2,1)S(1)} %copy-done, bf16[2,160,256]{2,1,0:T(8,128)(2,1)S(1)} %collective-permute-done.10.refs_1_, bf16[2,160,256]{2,1,0:T(8,128)(2,1)S(1)} %collective-permute-done.11.refs_2_, ...), custom_call_target="tpu_custom_call" | custom-call | flops 1677721600 | bytes 1966080 | tf_op jit(solution)/shard_map/attend/pallas_call | solution.py:142
  82.8 0.0 collective-permute-done.8.refs_1_
  82.8 0.0 collective-permute-done.9.refs_2_
  82.8 2.1 %attend.10 = (f32[640,256]{1,0:T(8,128)S(1)}, f32[640,256]{1,0:T(8,128)S(1)}, f32[640,256]{1,0:T(8,128)S(1)}) custom-call(bf16[640,256]{1,0:T(8,128)(2,1)S(1)} %copy-done, bf16[640,256]{1,0:T(8,128)(2,1)S(1)} %collective-permute-done.8.refs_1_, bf16[640,256]{1,0:T(8,128)(2,1)S(1)} %collective-permute-done.9.refs_2_, ...), custom_call_target="tpu_custom_call" | custom-call | flops 838860800 | bytes 1310720 | tf_op jit(solution)/shard_map/attend/pallas_call | solution.py:142
  84.9 10.6 %collective-permute-done.7.refs_4_ = bf16[256,256]{1,0:T(8,128)(2,1)S(1)} collective-permute-done((bf16[256,256]{1,0:T(8,128)(2,1)S(1)}, bf16[256,256]{1,0:T(8,128)(2,1)S(1)}, u32[]{:S(2)}, u32[]{:S(2)}) %collective-permute-start.7) | collective-permute-done | bytes 131104 | tf_op jit(solution)/shard_map/ppermute | solution.py:158
  95.5 4.0 %collective-permute-done.5.refs_3_ = bf16[384,256]{1,0:T(8,128)(2,1)S(1)} collective-permute-done((bf16[384,256]{1,0:T(8,128)(2,1)S(1)}, bf16[384,256]{1,0:T(8,128)(2,1)S(1)}, u32[]{:S(2)}, u32[]{:S(2)}) %collective-permute-start.5) | collective-permute-done | bytes 196640 | tf_op jit(solution)/shard_map/ppermute | solution.py:158
  99.6 0.0 collective-permute-done.3.refs_2_
  99.6 2.1 %attend.11 = bf16[640,256]{1,0:T(8,128)(2,1)S(1)} custom-call(bf16[640,256]{1,0:T(8,128)(2,1)S(1)} %copy-done, bf16[288,256]{1,0:T(8,128)(2,1)S(1)} %collective-permute-done.1.refs_1_, bf16[512,256]{1,0:T(8,128)(2,1)S(1)} %collective-permute-done.3.refs_2_, bf16[384,256]{1,0:T(8,128)(2,1)S(1)} %collective-permute-done.5.refs_3_, ...), custom_call_target="tpu_custom_call" | custom-call | flops 838860800 | bytes 1310720 | tf_op jit(solution)/shard_map/attend/pallas_call | solution.py:142
  101.6 12.9 %all_to_all.19 = bf16[8,80,256]{2,1,0:T(8,128)(2,1)S(1)} all-to-all(bf16[8,80,256]{2,1,0:T(8,128)(2,1)S(1)} %bitcast.8), channel_id=1, replica_groups=mesh['ctx'=32,'head'=8] {'head'}, dimensions={0} | all-to-all | bytes 655360 | tf_op jit(solution)/shard_map/all_to_all | solution.py:199
  114.5 0.8 copy.7
  (5 shorter events, 0.0 us)
Async XLA Ops:
  1.4 8.6 %collective-permute-start = (bf16[208,256]{1,0:T(8,128)(2,1)S(1)}, bf16[208,256]{1,0:T(8,128)(2,1)S(1)}, u32[]{:S(2)}, u32[]{:S(2)}) collective-permute-start(bf16[208,256]{1,0:T(8,128)(2,1)S(1)} %get-tuple-element.24.refs_1_), channel_id=1, source_target_pairs={{0,64},{8,72},{16,80},{24,88},{32,96},{40,104},{48,112},{56,120},{... | collective-permute-start | bytes 319496 | tf_op jit(solution)/shard_map/ppermute | solution.py:158
  10.0 58.7 %copy-start = (bf16[640,256]{1,0:T(8,128)(2,1)S(1)}, bf16[640,256]{1,0:T(8,128)(2,1)}, u32[]{:S(2)}) copy-start(bf16[640,256]{1,0:T(8,128)(2,1)} %refs_0_.11) | copy-start | bytes 983044
  10.0 8.4 %collective-permute-start.1 = (bf16[288,256]{1,0:T(8,128)(2,1)S(1)}, bf16[288,256]{1,0:T(8,128)(2,1)S(1)}, u32[]{:S(2)}, u32[]{:S(2)}) collective-permute-start(bf16[288,256]{1,0:T(8,128)(2,1)S(1)} %pad_maximum_fusion.1), channel_id=1, source_target_pairs={{0,192},{8,200},{16,208},{24,216},{32,224},{40,232},{48,240},{56,2... | collective-permute-start | bytes 442376 | tf_op jit(solution)/shard_map/ppermute | solution.py:158
  13.8 34.6 %collective-permute-start.19 = (bf16[640,256]{1,0:T(8,128)(2,1)}, bf16[640,256]{1,0:T(8,128)(2,1)S(1)}, u32[]{:S(2)}, u32[]{:S(2)}) collective-permute-start(bf16[640,256]{1,0:T(8,128)(2,1)} %keys.1), channel_id=1, source_target_pairs={{0,8},{8,0},{16,24},{24,16},{32,40},{40,32},{48,56},{56,48},{64,72... | collective-permute-start | bytes 983048 | tf_op jit(solution)/shard_map/ppermute | solution.py:158
  13.8 34.9 %collective-permute-start.20 = (bf16[640,256]{1,0:T(8,128)(2,1)}, bf16[640,256]{1,0:T(8,128)(2,1)S(1)}, u32[]{:S(2)}, u32[]{:S(2)}) collective-permute-start(bf16[640,256]{1,0:T(8,128)(2,1)} %values.1), channel_id=1, source_target_pairs={{0,8},{8,0},{16,24},{24,16},{32,40},{40,32},{48,56},{56,48},{64,72... | collective-permute-start | bytes 983048 | tf_op jit(solution)/shard_map/ppermute | solution.py:158
  14.4 33.1 %collective-permute-start.2 = (bf16[512,256]{1,0:T(8,128)(2,1)S(1)}, bf16[512,256]{1,0:T(8,128)(2,1)S(1)}, u32[]{:S(2)}, u32[]{:S(2)}) collective-permute-start(bf16[512,256]{1,0:T(8,128)(2,1)S(1)} %get-tuple-element.25.refs_2_), channel_id=1, source_target_pairs={{0,64},{8,72},{16,80},{24,88},{32,96},{40,104},{48,112},{56,120},{... | collective-permute-start | bytes 786440 | tf_op jit(solution)/shard_map/ppermute | solution.py:158
  17.7 26.5 %collective-permute-start.4 = (bf16[384,256]{1,0:T(8,128)(2,1)S(1)}, bf16[384,256]{1,0:T(8,128)(2,1)S(1)}, u32[]{:S(2)}, u32[]{:S(2)}) collective-permute-start(bf16[384,256]{1,0:T(8,128)(2,1)S(1)} %get-tuple-element.26.refs_3_), channel_id=1, source_target_pairs={{0,64},{8,72},{16,80},{24,88},{32,96},{40,104},{48,112},{56,120},{... | collective-permute-start | bytes 589832 | tf_op jit(solution)/shard_map/ppermute | solution.py:158
  18.4 25.5 %collective-permute-start.6 = (bf16[256,256]{1,0:T(8,128)(2,1)S(1)}, bf16[256,256]{1,0:T(8,128)(2,1)S(1)}, u32[]{:S(2)}, u32[]{:S(2)}) collective-permute-start(bf16[256,256]{1,0:T(8,128)(2,1)S(1)} %get-tuple-element.27.refs_4_), channel_id=1, source_target_pairs={{0,64},{8,72},{16,80},{24,88},{32,96},{40,104},{48,112},{56,120},{... | collective-permute-start | bytes 393224 | tf_op jit(solution)/shard_map/ppermute | solution.py:158
  43.9 12.3 %collective-permute-start.17 = (bf16[640,256]{1,0:T(8,128)(2,1)}, bf16[640,256]{1,0:T(8,128)(2,1)S(1)}, u32[]{:S(2)}, u32[]{:S(2)}) collective-permute-start(bf16[640,256]{1,0:T(8,128)(2,1)} %keys.1), channel_id=1, source_target_pairs={{0,16},{8,24},{16,0},{24,8},{32,48},{40,56},{48,32},{56,40},{64,80... | collective-permute-start | bytes 983048 | tf_op jit(solution)/shard_map/ppermute | solution.py:158
  44.3 19.0 %collective-permute-start.18 = (bf16[640,256]{1,0:T(8,128)(2,1)}, bf16[640,256]{1,0:T(8,128)(2,1)S(1)}, u32[]{:S(2)}, u32[]{:S(2)}) collective-permute-start(bf16[640,256]{1,0:T(8,128)(2,1)} %values.1), channel_id=1, source_target_pairs={{0,16},{8,24},{16,0},{24,8},{32,48},{40,56},{48,32},{56,40},{64,80... | collective-permute-start | bytes 983048 | tf_op jit(solution)/shard_map/ppermute | solution.py:158
  47.5 6.6 %collective-permute-start.10 = (bf16[2,160,256]{2,1,0:T(8,128)(2,1)S(1)}, bf16[2,160,256]{2,1,0:T(8,128)(2,1)S(1)}, u32[]{:S(2)}, u32[]{:S(2)}) collective-permute-start(bf16[2,160,256]{2,1,0:T(8,128)(2,1)S(1)} %pad_maximum_fusion.refs_1_), channel_id=1, source_target_pairs={{0,224},{8,232},{16,240},{24,248},{32,64},{40,72},{48,80},{56,88},... | collective-permute-start | bytes 491528 | tf_op jit(solution)/shard_map/ppermute | solution.py:158
  48.4 18.3 %collective-permute-start.14 = (bf16[2,160,256]{2,1,0:T(8,128)(2,1)S(1)}, bf16[2,160,256]{2,1,0:T(8,128)(2,1)S(1)}, u32[]{:S(2)}, u32[]{:S(2)}) collective-permute-start(bf16[2,160,256]{2,1,0:T(8,128)(2,1)S(1)} %pad_maximum_fusion.refs_1_), channel_id=1, source_target_pairs={{0,16},{8,24},{16,0},{24,8},{32,48},{40,56},{48,32},{56,40},{64,80... | collective-permute-start | bytes 491528 | tf_op jit(solution)/shard_map/ppermute | solution.py:158
  48.8 18.0 %collective-permute-start.15 = (bf16[2,160,256]{2,1,0:T(8,128)(2,1)S(1)}, bf16[2,160,256]{2,1,0:T(8,128)(2,1)S(1)}, u32[]{:S(2)}, u32[]{:S(2)}) collective-permute-start(bf16[2,160,256]{2,1,0:T(8,128)(2,1)S(1)} %pad_maximum_fusion.refs_1_), channel_id=1, source_target_pairs={{0,8},{8,0},{16,24},{24,16},{32,40},{40,32},{48,56},{56,48},{64,72... | collective-permute-start | bytes 491528 | tf_op jit(solution)/shard_map/ppermute | solution.py:158
  54.1 14.6 %collective-permute-start.11 = (bf16[2,160,256]{2,1,0:T(8,128)(2,1)S(1)}, bf16[2,160,256]{2,1,0:T(8,128)(2,1)S(1)}, u32[]{:S(2)}, u32[]{:S(2)}) collective-permute-start(bf16[2,160,256]{2,1,0:T(8,128)(2,1)S(1)} %collective-permute-done.10.refs_1_), channel_id=1, source_target_pairs={{0,16},{8,24},{16,0},{24,8},{32,48},{40,56},{48,32},{56,40},{64,80... | collective-permute-start | bytes 491528 | tf_op jit(solution)/shard_map/ppermute | solution.py:158
  56.2 26.6 %collective-permute-start.8 = (bf16[640,256]{1,0:T(8,128)(2,1)}, bf16[640,256]{1,0:T(8,128)(2,1)S(1)}, u32[]{:S(2)}, u32[]{:S(2)}) collective-permute-start(bf16[640,256]{1,0:T(8,128)(2,1)} %keys.1), channel_id=1, source_target_pairs={{0,32},{8,40},{16,48},{24,56},{32,0},{40,8},{48,16},{56,24},{64,96... | collective-permute-start | bytes 983048 | tf_op jit(solution)/shard_map/ppermute | solution.py:158
  63.2 19.6 %collective-permute-start.9 = (bf16[640,256]{1,0:T(8,128)(2,1)}, bf16[640,256]{1,0:T(8,128)(2,1)S(1)}, u32[]{:S(2)}, u32[]{:S(2)}) collective-permute-start(bf16[640,256]{1,0:T(8,128)(2,1)} %values.1), channel_id=1, source_target_pairs={{0,32},{8,40},{16,48},{24,56},{32,0},{40,8},{48,16},{56,24},{64,96... | collective-permute-start | bytes 983048 | tf_op jit(solution)/shard_map/ppermute | solution.py:158
  66.7 8.7 %collective-permute-start.12 = (bf16[2,160,256]{2,1,0:T(8,128)(2,1)S(1)}, bf16[2,160,256]{2,1,0:T(8,128)(2,1)S(1)}, u32[]{:S(2)}, u32[]{:S(2)}) collective-permute-start(bf16[2,160,256]{2,1,0:T(8,128)(2,1)S(1)} %collective-permute-done.10.refs_1_), channel_id=1, source_target_pairs={{0,8},{8,0},{16,24},{24,16},{32,40},{40,32},{48,56},{56,48},{64,72... | collective-permute-start | bytes 491528 | tf_op jit(solution)/shard_map/ppermute | solution.py:158
  66.8 6.5 %collective-permute-start.16 = (bf16[2,160,256]{2,1,0:T(8,128)(2,1)S(1)}, bf16[2,160,256]{2,1,0:T(8,128)(2,1)S(1)}, u32[]{:S(2)}, u32[]{:S(2)}) collective-permute-start(bf16[2,160,256]{2,1,0:T(8,128)(2,1)S(1)} %collective-permute-done.14.refs_2_), channel_id=1, source_target_pairs={{0,8},{8,0},{16,24},{24,16},{32,40},{40,32},{48,56},{56,48},{64,72... | collective-permute-start | bytes 491528 | tf_op jit(solution)/shard_map/ppermute | solution.py:158
  68.7 11.0 %collective-permute-start.13 = (bf16[2,160,256]{2,1,0:T(8,128)(2,1)S(1)}, bf16[2,160,256]{2,1,0:T(8,128)(2,1)S(1)}, u32[]{:S(2)}, u32[]{:S(2)}) collective-permute-start(bf16[2,160,256]{2,1,0:T(8,128)(2,1)S(1)} %collective-permute-done.11.refs_2_), channel_id=1, source_target_pairs={{0,8},{8,0},{16,24},{24,16},{32,40},{40,32},{48,56},{56,48},{64,72... | collective-permute-start | bytes 491528 | tf_op jit(solution)/shard_map/ppermute | solution.py:158
  73.3 26.3 %collective-permute-start.3 = (bf16[512,256]{1,0:T(8,128)(2,1)S(1)}, bf16[512,256]{1,0:T(8,128)(2,1)S(1)}, u32[]{:S(2)}, u32[]{:S(2)}) collective-permute-start(bf16[512,256]{1,0:T(8,128)(2,1)S(1)} %collective-permute-done.2.refs_6_), channel_id=1, source_target_pairs={{0,192},{8,200},{16,208},{24,216},{32,224},{40,232},{48,240},{56,2... | collective-permute-start | bytes 786440 | tf_op jit(solution)/shard_map/ppermute | solution.py:158
  75.5 20.1 %collective-permute-start.7 = (bf16[256,256]{1,0:T(8,128)(2,1)S(1)}, bf16[256,256]{1,0:T(8,128)(2,1)S(1)}, u32[]{:S(2)}, u32[]{:S(2)}) collective-permute-start(bf16[256,256]{1,0:T(8,128)(2,1)S(1)} %collective-permute-done.6.refs_8_), channel_id=1, source_target_pairs={{0,192},{8,200},{16,208},{24,216},{32,224},{40,232},{48,240},{56,2... | collective-permute-start | bytes 393224 | tf_op jit(solution)/shard_map/ppermute | solution.py:158
  79.7 19.9 %collective-permute-start.5 = (bf16[384,256]{1,0:T(8,128)(2,1)S(1)}, bf16[384,256]{1,0:T(8,128)(2,1)S(1)}, u32[]{:S(2)}, u32[]{:S(2)}) collective-permute-start(bf16[384,256]{1,0:T(8,128)(2,1)S(1)} %collective-permute-done.4.refs_7_), channel_id=1, source_target_pairs={{0,192},{8,200},{16,208},{24,216},{32,224},{40,232},{48,240},{56,2... | collective-permute-start | bytes 589832 | tf_op jit(solution)/shard_map/ppermute | solution.py:158
